TPU v7x, 32 devices: a whole 2x2x4 slice. The times are simulated.
32 devices in a mesh: blk: 8 (over z, core), pair: 2 (over x), head: 2 (over y).
Axes of the slice: x: 2, y: 2, z: 4, core: 2. Of those that a mesh axis runs over, the one named last changes fastest.
Arguments:
- prefix_query_rows: bfloat16 [1024, 8, 8, 128], P('blk', 'head', 'pair'), may hold values from -6 to 6
- prefix_key_rows: bfloat16 [1024, 8, 128], P('blk', 'head'), may hold values from -6 to 6
- prefix_value_rows: bfloat16 [1024, 8, 128], P('blk', 'head'), may hold values from -6 to 6
- prefix_output_gradient: bfloat16 [1024, 8, 8, 128], P('blk', 'head', 'pair'), may hold values from -6 to 6
- resp_q: bfloat16 [2, 1024, 8, 8, 128], P('pair', 'blk', 'head'), may hold values from -100 to 100
- resp_k: bfloat16 [2, 1024, 8, 128], P('pair', 'blk', 'head'), may hold values from -4 to 4
- response_value_rows: bfloat16 [2, 1024, 8, 128], P('pair', 'blk', 'head'), may hold values from -6 to 6
- response_output_gradient: bfloat16 [2, 1024, 8, 8, 128], P('pair', 'blk', 'head'), may hold values from -6 to 6
- lengths: int32 [2], replicated, may hold values from 128 to 1024, as said below
- prefix_order: int32 [8], replicated, may hold values from 0 to 7, each once
Outputs:
- dprefix_q: bfloat16 [1024, 8, 8, 128], P(('blk', 'head'), None, 'pair')
- dprefix_k: bfloat16 [1024, 8, 128], P(('blk', 'head'))
- dprefix_v: bfloat16 [1024, 8, 128], P(('blk', 'head'))
- dresp_q: bfloat16 [2, 1024, 8, 8, 128], P('pair', ('blk', 'head'))
- dresp_k: bfloat16 [2, 1024, 8, 128], P('pair', ('blk', 'head'))
- dresp_v: bfloat16 [2, 1024, 8, 128], P('pair', ('blk', 'head'))
Inputs may be any that keep to these rules, and one draw needn't show every extreme that they name: `prefix_order`: the stored prefix blocks are the prefix blocks 0 to 7, each once. Each length is a multiple of 128; one of the two lengths equals 1024.
All inputs are finite; a program needn't handle non-finite values.
Results may differ from a plain program's by a relative error of at most 0.0051.
Values may be sent and summed in bfloat16 or wider, within the bound.
No kernel may reach another device: no remote copies, remote signals or barrier semaphores. Data moves between devices by JAX's collectives and lax.ppermute only.
A program may use at most 192 MiB of HBM per device.

v0:
```python
import jax
import jax.numpy as jnp
from jax import lax
from jax.sharding import PartitionSpec as P

PBLK = 128


very_low = -1e30


def on_device(
    prefix_query_rows,
    prefix_key_rows,
    prefix_value_rows,
    prefix_output_gradient,
    resp_q,
    resp_k,
    response_value_rows,
    response_output_gradient,
    lengths,
    prefix_order,
):
    cycle_size = lax.axis_size("blk")
    cycle_index = lax.axis_index("blk")
    pair_index = lax.axis_index("pair")
    pref_rows = prefix_key_rows.shape[0]
    local_heads = prefix_key_rows.shape[1]
    head_size = prefix_key_rows.shape[2]
    half_heads = prefix_query_rows.shape[2]
    resp_rows = resp_k.shape[1]
    all_heads = resp_q.shape[3]
    block_rows = pref_rows + resp_rows
    prefix_total = pref_rows * cycle_size
    scaling = head_size ** (-0.5)
    slot_table = jnp.arange(prefix_order.shape[0], dtype=jnp.int32)

    def key_positions(begin_row, row_count):
        row_index = begin_row + jnp.arange(row_count, dtype=jnp.int32)
        owners = row_index // block_rows
        offset = row_index % block_rows
        slot_ids = owners * (pref_rows // PBLK) + jnp.minimum(offset, pref_rows - 1) // PBLK
        chosen = jnp.sum(
            jnp.where(slot_ids[:, None] == slot_table[None, :], prefix_order[None, :], 0), axis=1
        )
        prefix_pos = chosen * PBLK + offset % PBLK
        resp_pos = prefix_total + owners * resp_rows + offset - pref_rows
        return jnp.where(offset < pref_rows, prefix_pos, resp_pos)

    own_prefix = key_positions(cycle_index * block_rows, pref_rows)
    own_resp = prefix_total + cycle_index * resp_rows + jnp.arange(resp_rows, dtype=jnp.int32)
    query_pos = jnp.concatenate(
        [jnp.repeat(own_prefix, half_heads), jnp.repeat(own_resp, all_heads)]
    )
    live_len = jnp.sum(jnp.where(jnp.arange(2) == pair_index, lengths, 0))
    live_rows = own_resp - prefix_total < live_len
    resp_douts = jnp.where(
        live_rows[:, None, None, None], response_output_gradient[0], jnp.zeros((), jnp.bfloat16)
    )
    queries = jnp.concatenate(
        [
            prefix_query_rows.transpose(1, 0, 2, 3).reshape(local_heads, -1, head_size),
            resp_q[0].transpose(1, 0, 2, 3).reshape(local_heads, -1, head_size),
        ],
        axis=1,
    )
    grad_outs = jnp.concatenate(
        [
            prefix_output_gradient.transpose(1, 0, 2, 3).reshape(local_heads, -1, head_size),
            resp_douts.transpose(1, 0, 2, 3).reshape(local_heads, -1, head_size),
        ],
        axis=1,
    )
    key_value = jnp.stack(
        [
            jnp.concatenate([prefix_key_rows, resp_k[0]], axis=0),
            jnp.concatenate([prefix_value_rows, response_value_rows[0]], axis=0),
        ]
    ).transpose(0, 2, 1, 3)
    query_rows = queries.shape[1]

    def scores_of(pieces, begin_row):
        visible = (
            key_positions(begin_row, pieces.shape[2])[None, None, :] <= query_pos[None, :, None]
        )
        logits = (
            jnp.einsum("gqd,gkd->gqk", queries, pieces[0], preferred_element_type=jnp.float32)
            * scaling
        )
        dprobs = jnp.einsum(
            "gqd,gkd->gqk", grad_outs, pieces[1], preferred_element_type=jnp.float32
        )
        return (logits, dprobs, visible)

    running_max = jnp.full((local_heads, query_rows), very_low, jnp.float32)
    logits, dprobs, visible = scores_of(
        lax.all_gather(key_value, "blk", axis=2, tiled=True), jnp.int32(0)
    )
    new_max = jnp.maximum(running_max, jnp.max(jnp.where(visible, logits, very_low), axis=2))
    weights = jnp.where(visible, jnp.exp(logits - new_max[:, :, None]), 0.0)
    running_sum = jnp.sum(weights, axis=2)
    running_dot = jnp.sum(weights * dprobs, axis=2)
    log_total = new_max + jnp.log(running_sum)
    deltas = running_dot / running_sum
    pieces = lax.all_gather(key_value, "blk", axis=2, tiled=True)
    logits, dprobs, visible = scores_of(pieces, jnp.int32(0))
    softmax = jnp.where(visible, jnp.exp(logits - log_total[:, :, None]), 0.0)
    dscores = (softmax * (dprobs - deltas[:, :, None]) * scaling).astype(jnp.bfloat16)
    soft_bf = softmax.astype(jnp.bfloat16)
    dq_term = jnp.einsum("gqk,gkd->gqd", dscores, pieces[0], preferred_element_type=jnp.float32)
    dk_term = jnp.einsum("gqk,gqd->gkd", dscores, queries, preferred_element_type=jnp.float32)
    dv_term = jnp.einsum("gqk,gqd->gkd", soft_bf, grad_outs, preferred_element_type=jnp.float32)
    dq_term, kv_term = (dq_term, jnp.stack([dk_term, dv_term]))
    kv_grads = lax.psum_scatter(kv_term, "blk", scatter_dimension=2, tiled=True)
    split_row = pref_rows * half_heads
    dq_pref = (
        dq_term[:, :split_row]
        .reshape(local_heads, pref_rows, half_heads, head_size)
        .transpose(1, 0, 2, 3)
        .astype(jnp.bfloat16)
    )
    dq_resp = (
        dq_term[:, split_row:]
        .reshape(local_heads, resp_rows, all_heads, head_size)
        .transpose(1, 0, 2, 3)
        .astype(jnp.bfloat16)
    )
    pref_grads = kv_grads[:, :, :pref_rows].transpose(0, 2, 1, 3)
    resp_grads = kv_grads[:, :, pref_rows:].transpose(0, 2, 1, 3).astype(jnp.bfloat16)
    summed = lax.psum(pref_grads, "pair").astype(jnp.bfloat16)
    prefix_dq, prefix_dk, prefix_dv, resp_dq, resp_dk, resp_dv = (
        lax.all_to_all(dq_pref, "head", split_axis=0, concat_axis=1, tiled=True),
        lax.all_to_all(summed[0], "head", split_axis=0, concat_axis=1, tiled=True),
        lax.all_to_all(summed[1], "head", split_axis=0, concat_axis=1, tiled=True),
        lax.all_to_all(dq_resp, "head", split_axis=0, concat_axis=1, tiled=True),
        lax.all_to_all(resp_grads[0], "head", split_axis=0, concat_axis=1, tiled=True),
        lax.all_to_all(resp_grads[1], "head", split_axis=0, concat_axis=1, tiled=True),
    )
    return (prefix_dq, prefix_dk, prefix_dv, resp_dq[None], resp_dk[None], resp_dv[None])


def solution(mesh):
    in_specs = (
        P("blk", "head", "pair", None),
        P("blk", "head", None),
        P("blk", "head", None),
        P("blk", "head", "pair", None),
        P("pair", "blk", "head", None, None),
        P("pair", "blk", "head", None),
        P("pair", "blk", "head", None),
        P("pair", "blk", "head", None, None),
        P(),
        P(),
    )
    out_specs = (
        P(("blk", "head"), None, "pair", None),
        P(("blk", "head"), None, None),
        P(("blk", "head"), None, None),
        P("pair", ("blk", "head"), None, None, None),
        P("pair", ("blk", "head"), None, None),
        P("pair", ("blk", "head"), None, None),
    )
    return jax.shard_map(
        on_device, mesh=mesh, in_specs=in_specs, out_specs=out_specs, check_vma=False
    )
```

profile of v0, /device:TPU:0, one launch (start us, length us, event | category | flops | bytes accessed | tf_op | source)
XLA Modules:
  0.0 363.4 jit_solution(13658420740939795144)
XLA Ops:
  7.2 1.0 copy.73
  8.2 0.9 copy.75
  9.2 0.9 copy.102
  10.1 0.9 copy.101
  11.1 0.8 maximum_bitcast_fusion
  12.0 0.7 select_reduce_fusion.2
  13.2 1.2 copy.70
  14.4 1.2 copy.76
  15.6 1.3 fusion.31
  16.9 0.7 add_compare_fusion
  17.6 0.7 select_reduce_fusion.1
  18.4 0.2 copy_bitcast_fusion.2
  18.6 1.5 copy_bitcast_fusion.1
  20.1 3.4 broadcast_compare_fusion
  23.5 38.2 %all-gather.2.cloned.1.call-done = bf16[2,4,2048,128]{3,2,1,0:T(8,128)(2,1)} async-done(((bf16[2,4,256,128]{3,2,1,0:T(8,128)(2,1)}), bf16[2,4,2048,128]{3,2,1,0:T(8,128)(2,1)}) %all-gather.2.cloned.1.call-update) | async-done | bytes 4194320 | tf_op jit(solution)/shard_map/all_gather | solution.py:105
  61.7 22.2 %select_reduce_fusion = (f32[4,1536]{1,0:T(4,128)S(1)}, f32[4,1536,2048]{2,1,0:T(8,128)}) fusion(pred[1536,2048]{1,0:T(8,128)(4,1)} %broadcast_compare_fusion, bf16[2,4,2048,128]{3,2,1,0:T(8,128)(2,1)} %all-gather.2.cloned.1.call-done, bf16[4,1024,128]{2,1,0:T(8,128)(2,1)S(1)} %copy_bitcast_fusion.2, bf16[4,512,128]{2,1,0:T(8,128)(2,1)S(1)} %bitcast.96), kind=kOutput, calls=%fused_computation.4 | convolution fusion | flops 3262113792 | bytes 57171968 | tf_op jit(solution)/shard_map/gqd,gkd->gqk/dot_general | solution.py:87
  83.9 40.0 %fusion = (f32[4,1536]{1,0:T(4,128)S(1)}, f32[4,1536]{1,0:T(4,128)S(1)}, f32[4,1536,2048]{2,1,0:T(8,128)}) fusion(f32[4,1536,2048]{2,1,0:T(8,128)} %get-tuple-element.15, f32[4,1536]{1,0:T(4,128)S(1)} %broadcast_maximum_fusion, pred[1536,2048]{1,0:T(8,128)(4,1)S(1)} %copy-done.2, bf16[2,4,2048,128]{3,2,1,0:T(8,128)(2,1)} %all-gather.2.cloned.1.call-done, ...), kind=kOutput, calls=%fused_computation.5 | convolution fusion | flops 3299856384 | bytes 107552768 | tf_op jit(solution)/shard_map/gqd,gkd->gqk/dot_general | solution.py:90
  124.0 24.4 %fusion.5 = f32[1,4,2048,128]{3,2,1,0:T(8,128)} fusion(f32[4,1536,2048]{2,1,0:T(8,128)} %get-tuple-element.15, f32[4,1536]{1,0:T(4,128)S(1)} %get-tuple-element.12, pred[1536,2048]{1,0:T(8,128)(4,1)S(1)} %copy-done.2, bf16[4,1024,128]{2,1,0:T(8,128)(2,1)S(1)} %copy_bitcast_fusion.1, bf16[4,512,128]{2,1,0:T(8,128)(2,1)S(1)} %bitcast.104), kind=kOutput, calls=%fused_computation.11 | convolution fusion | flops 3274702848 | bytes 59269120 | tf_op jit(solution)/shard_map/gqk,gqd->gkd/dot_general | solution.py:112
  148.3 41.1 %multiply_convert_fusion = bf16[4,1536,2048]{2,1,0:T(8,128)(2,1)} fusion(f32[4,1536,2048]{2,1,0:T(8,128)} %get-tuple-element.16, f32[4,1536,2048]{2,1,0:T(8,128)} %get-tuple-element.15, f32[4,1536]{1,0:T(4,128)S(1)} %get-tuple-element.13, f32[4,1536]{1,0:T(4,128)S(1)} %get-tuple-element.12, pred[1536,2048]{1,0:T(8,128)(4,1)} %broadcast_compare_fusion), kind=kLoop, calls=%fused_computation | loop fusion | flops 88080384 | bytes 129024000 | tf_op jit(solution)/shard_map/convert_element_type | solution.py:108
  189.5 15.9 %convolution_bitcast_fusion = f32[1,4,2048,128]{3,2,1,0:T(8,128)} fusion(bf16[4,1536,2048]{2,1,0:T(8,128)(2,1)} %multiply_convert_fusion, bf16[4,1024,128]{2,1,0:T(8,128)(2,1)S(1)} %copy_bitcast_fusion.2, bf16[4,512,128]{2,1,0:T(8,128)(2,1)S(1)} %bitcast.97), kind=kOutput, calls=%fused_computation.12 | convolution fusion | flops 3224371200 | bytes 30932992 | tf_op jit(solution)/shard_map/gqk,gqd->gkd/dot_general | solution.py:111
  205.3 7.3 %pad_maximum_fusion = f32[2,4,2048,128]{3,2,1,0:T(8,128)} fusion(f32[1,4,2048,128]{3,2,1,0:T(8,128)} %fusion.5, f32[1,4,2048,128]{3,2,1,0:T(8,128)} %convolution_bitcast_fusion), kind=kLoop, calls=%fused_computation.9 | loop fusion | flops 2097152 | bytes 16777216 | tf_op jit(solution)/shard_map/stack | solution.py:113
  212.7 13.1 %convolution_convert_fusion = bf16[4,1536,128]{2,1,0:T(8,128)(2,1)S(1)} fusion(bf16[4,1536,2048]{2,1,0:T(8,128)(2,1)} %multiply_convert_fusion, bf16[2,4,2048,128]{3,2,1,0:T(8,128)(2,1)} %all-gather.2.cloned.1.call-done), kind=kOutput, calls=%fused_computation.13 | convolution fusion | flops 3222011904 | bytes 28835840 | tf_op jit(solution)/shard_map/gqk,gkd->gqd/dot_general | solution.py:110
  225.8 1.2 copy.100
  227.1 3.5 all-to-all-start
  230.6 2.4 copy_bitcast_fusion
  233.0 68.1 %reduce-scatter.2.cloned.1.call-done = f32[2,4,256,128]{3,2,1,0:T(8,128)} async-done(((f32[2,4,2048,128]{3,2,1,0:T(8,128)}), f32[2,4,256,128]{3,2,1,0:T(8,128)}) %reduce-scatter.2.cloned.1.call-update) | async-done | bytes 1048592 | tf_op jit(solution)/shard_map/reduce_scatter | solution.py:114
  301.1 1.1 slice_bitcast_fusion.6
  302.2 1.1 fusion.11
  303.3 0.8 copy.90
  304.1 3.6 all-to-all-start.3
  307.7 15.8 %all-reduce.1 = bf16[2,128,4,128]{3,1,2,0:T(8,128)(2,1)S(1)} all-reduce(f32[2,128,4,128]{3,1,2,0:T(8,128)S(1)} %slice_bitcast_fusion.6), channel_id=1, replica_groups=mesh['blk'=8,'pair'=2,'head'=2] {'pair'}, use_global_device_ids=true, to_apply=%region_7.8 | all-reduce | flops 131072 | bytes 786432 | tf_op jit(solution)/shard_map/psum | solution.py:130
  323.5 3.6 all-to-all-start.5
  327.1 0.8 copy.84
  327.8 3.8 %all-to-all-done.5 = bf16[128,4,128]{2,1,0:T(4,128)(2,1)S(1)} async-done(((bf16[128,4,128]{2,1,0:T(4,128)(2,1)}), bf16[128,4,128]{2,1,0:T(4,128)(2,1)S(1)}, u32[]{:S(2)}, u32[]{:S(2)}) %all-to-all-start.5) | async-done | bytes 131104 | tf_op jit(solution)/shard_map/all_to_all | solution.py:137
  331.6 3.4 all-to-all-start.2
  335.0 0.8 copy.88
  335.7 4.4 %all-to-all-done.2 = bf16[128,4,128]{2,1,0:T(4,128)(2,1)S(1)} async-done(((bf16[128,4,128]{2,1,0:T(4,128)(2,1)}), bf16[128,4,128]{2,1,0:T(4,128)(2,1)S(1)}, u32[]{:S(2)}, u32[]{:S(2)}) %all-to-all-start.2) | async-done | bytes 131104 | tf_op jit(solution)/shard_map/all_to_all | solution.py:134
  340.1 3.4 all-to-all-start.4
  343.5 0.8 copy.82
  344.3 3.7 %all-to-all-done.4 = bf16[128,4,128]{2,1,0:T(4,128)(2,1)S(1)} async-done(((bf16[128,4,128]{2,1,0:T(4,128)(2,1)}), bf16[128,4,128]{2,1,0:T(4,128)(2,1)S(1)}, u32[]{:S(2)}, u32[]{:S(2)}) %all-to-all-start.4) | async-done | bytes 131104 | tf_op jit(solution)/shard_map/all_to_all | solution.py:136
  348.0 3.4 all-to-all-start.1
  351.3 1.0 copy.79
  352.3 1.1 copy.87
  353.4 0.7 copy.91
  354.2 0.7 copy.85
  354.9 0.7 copy.89
  355.6 0.3 all-to-all-done.1
  355.8 0.7 copy.83
  (30 shorter events, 0.8 us)
Async XLA Ops:
  7.2 11.2 %copy-start = (bf16[1,128,4,8,128]{4,3,2,1,0:T(8,128)(2,1)S(1)}, bf16[1,128,4,8,128]{4,3,2,1,0:T(8,128)(2,1)}, u32[]{:S(2)}) copy-start(bf16[1,128,4,8,128]{4,3,2,1,0:T(8,128)(2,1)} %param.14) | copy-start | bytes 3145732
  7.2 54.5 %all-gather.2.cloned.1.call-start = ((), (), s32[]{:S(2)}) async-start(), calls=%async_computation.7 | async-start | bytes 4718592 | tf_op jit(solution)/shard_map/all_gather | solution.py:105
  11.9 289.2 %reduce-scatter.2.cloned.1.call-start = ((), (), s32[]{:S(2)}) async-start(), calls=%async_computation.8 | async-start | bytes 9437184 | tf_op jit(solution)/shard_map/reduce_scatter | solution.py:114
  61.7 22.2 %copy-start.2 = (pred[1536,2048]{1,0:T(8,128)(4,1)S(1)}, pred[1536,2048]{1,0:T(8,128)(4,1)}, u32[]{:S(2)}) copy-start(pred[1536,2048]{1,0:T(8,128)(4,1)} %broadcast_compare_fusion) | copy-start | bytes 9437188
  212.7 143.9 %copy-start.1 = (bf16[1,128,4,8,128]{4,3,2,1,0:T(8,128)(2,1)S(1)}, bf16[1,128,4,8,128]{4,3,2,1,0:T(8,128)(2,1)}, u32[]{:S(2)}) copy-start(bf16[1,128,4,8,128]{4,3,2,1,0:T(8,128)(2,1)} %param.14) | copy-start | bytes 3145732
  225.7 1.4 copy-start.3
  227.1 77.0 %all-to-all-start = ((bf16[128,4,4,128]{3,2,1,0:T(4,128)(2,1)}), bf16[128,4,4,128]{3,2,1,0:T(4,128)(2,1)S(1)}, u32[]{:S(2)}, u32[]{:S(2)}) async-start(bf16[128,4,4,128]{3,2,1,0:T(4,128)(2,1)} %bitcast.92), calls=%async_computation | async-start | bytes 1048576 | tf_op jit(solution)/shard_map/all_to_all | solution.py:132
  304.1 19.4 %all-to-all-start.3 = ((bf16[128,4,8,128]{3,2,1,0:T(8,128)(2,1)}), bf16[128,4,8,128]{3,2,1,0:T(8,128)(2,1)S(1)}, u32[]{:S(2)}, u32[]{:S(2)}) async-start(bf16[128,4,8,128]{3,2,1,0:T(8,128)(2,1)} %copy_bitcast_fusion), calls=%async_computation.4 | async-start | bytes 2097152 | tf_op jit(solution)/shard_map/all_to_all | solution.py:135
  323.5 8.1 %all-to-all-start.5 = ((bf16[128,4,128]{2,1,0:T(4,128)(2,1)}), bf16[128,4,128]{2,1,0:T(4,128)(2,1)S(1)}, u32[]{:S(2)}, u32[]{:S(2)}) async-start(bf16[128,4,128]{2,1,0:T(4,128)(2,1)} %copy.90), calls=%async_computation.6 | async-start | bytes 262144 | tf_op jit(solution)/shard_map/all_to_all | solution.py:137
  331.6 8.5 %all-to-all-start.2 = ((bf16[128,4,128]{2,1,0:T(4,128)(2,1)}), bf16[128,4,128]{2,1,0:T(4,128)(2,1)S(1)}, u32[]{:S(2)}, u32[]{:S(2)}) async-start(bf16[128,4,128]{2,1,0:T(4,128)(2,1)} %copy.84), calls=%async_computation.3 | async-start | bytes 262144 | tf_op jit(solution)/shard_map/all_to_all | solution.py:134
  340.1 7.8 %all-to-all-start.4 = ((bf16[128,4,128]{2,1,0:T(4,128)(2,1)}), bf16[128,4,128]{2,1,0:T(4,128)(2,1)S(1)}, u32[]{:S(2)}, u32[]{:S(2)}) async-start(bf16[128,4,128]{2,1,0:T(4,128)(2,1)} %copy.88), calls=%async_computation.5 | async-start | bytes 262144 | tf_op jit(solution)/shard_map/all_to_all | solution.py:136
  348.0 7.8 %all-to-all-start.1 = ((bf16[128,4,128]{2,1,0:T(4,128)(2,1)}), bf16[128,4,128]{2,1,0:T(4,128)(2,1)S(1)}, u32[]{:S(2)}, u32[]{:S(2)}) async-start(bf16[128,4,128]{2,1,0:T(4,128)(2,1)} %copy.82), calls=%async_computation.2 | async-start | bytes 262144 | tf_op jit(solution)/shard_map/all_to_all | solution.py:133
Sparse Core Ops, SparseCore 0:
  12.1 49.5 all-gather.1
  212.8 88.3 reduce-scatter.1
where the time goes:
time: 365 us; the launch traced here: 363 us
  waiting for transfers between devices  118 us (32%)
  matrix products  116 us (32%)
  other arithmetic  57.8 us (16%)
  starting transfers between devices  20.8 us (6%)
  local copies, waits for them, and re-layouts  20.7 us (6%)
  blocking collectives  15.8 us (4%)
  between operations  14.3 us (4%)
    reduce_scatter x1, waiting for transfers between devices, on_device(): kv_grads = lax.psum_scatter(kv_term, 'blk', scatter_dimension=2, tiled=True)  68.1 us
    convert_element_type x1, other arithmetic, on_device(): (softmax * (dprobs - deltas[:, :, None]) * scaling).astype(jnp.bfloat16)  41.1 us
    dot_general x1, matrix products, scores_of(): jnp.einsum('gqd,gkd->gqk', grad_outs, pieces[1], preferred_element_type=j...  40 us
    all_gather x1, waiting for transfers between devices, on_device(): pieces = lax.all_gather(key_value, 'blk', axis=2, tiled=True)  38.2 us
    dot_general x1, matrix products, on_device(): jnp.einsum('gqk,gqd->gkd', soft_bf, grad_outs, preferred_element_type=jnp...  24.4 us
    dot_general x1, matrix products, scores_of(): jnp.einsum('gqd,gkd->gqk', queries, pieces[0], preferred_element_type=jnp...  22.2 us
    dot_general x1, matrix products, on_device(): jnp.einsum('gqk,gqd->gkd', dscores, queries, preferred_element_type=jnp.f...  15.9 us
    psum x1, blocking collectives, on_device(): summed = lax.psum(pref_grads, 'pair').astype(jnp.bfloat16)  15.8 us
  transfers between devices with their start and end apart: 8, of which 6 were waited for; matrix products, arithmetic and copies ran while one was open for 10% of the time, Pallas kernels for 0%

commit v1 on v0

v1 whole, which is shorter than its diff:
```python
import functools
import math

import jax
import jax.numpy as jnp
from jax import lax
from jax.experimental import pallas as pl
from jax.experimental.pallas import tpu as pltpu
from jax.sharding import Mesh, PartitionSpec as P

F32 = jnp.float32
BF16 = jnp.bfloat16
very_low = -1e30


def dot_nt(a, b):
    return lax.dot_general(a, b, (((1,), (1,)), ((), ())), preferred_element_type=F32)


def dot_nn(a, b):
    return lax.dot_general(a, b, (((1,), (0,)), ((), ())), preferred_element_type=F32)


def dot_tn(a, b):
    return lax.dot_general(a, b, (((0,), (0,)), ((), ())), preferred_element_type=F32)


def attn_kernel(
    order,
    lengths,
    qp_ref,
    qr_ref,
    dop_ref,
    dor_ref,
    kv_ref,
    dq_ref,
    dkv_ref,
    q_sc,
    do_sc,
    k_sc,
    v_sc,
    dk_sc,
    dv_sc,
    e_sc,
    p_sc,
    m_sc,
    *,
    blocks,
    slots,
    rows,
    half,
    full,
    chunk,
    first_block,
    side,
):
    step = pl.program_id(1)
    tile = rows * half
    per_slot = 1 + full // half
    slot = step // per_slot
    part = step % per_slot
    head_size = qp_ref.shape[-1]
    scaling = head_size**-0.5
    cexp = scaling * math.log2(math.e)
    total = blocks * rows
    block = first_block() + slot

    @pl.when(step == 0)
    def _():
        for j in range(blocks):
            at = pl.multiple_of(order[j] * rows, rows)
            k_sc[pl.ds(at, rows), :] = kv_ref[j, 0, 0, :rows, :]
            v_sc[pl.ds(at, rows), :] = kv_ref[j, 1, 0, :rows, :]
            k_sc[pl.ds(total + j * rows, rows), :] = kv_ref[j, 0, 0, rows:, :]
            v_sc[pl.ds(total + j * rows, rows), :] = kv_ref[j, 1, 0, rows:, :]
        dk_sc[...] = jnp.zeros_like(dk_sc)
        dv_sc[...] = jnp.zeros_like(dv_sc)

    @pl.when(part == 0)
    def _():
        q_sc[...] = qp_ref[0, 0]
        do_sc[...] = dop_ref[0, 0]

    @pl.when(part > 0)
    def _():
        q_sc[...] = qr_ref[0, 0]
        do_sc[...] = dor_ref[0, 0]

    sub = tile // full
    pos0 = jnp.where(part == 0, order[block] * rows, total + block * rows + (part - 1) * sub)
    shift = jnp.where(part == 0, int(math.log2(half)), int(math.log2(full)))
    live = jnp.logical_or(part == 0, block * rows < lengths[side()])
    nfull = (pos0 + 1) // chunk

    def run():
        q = q_sc[...]
        do = do_sc[...]

        def scores(c, carry, masked):
            m, l, dl = carry
            base = pl.multiple_of(c * chunk, chunk)
            s = dot_nt(k_sc[pl.ds(base, chunk), :], q) * cexp
            if masked:
                kp = base + lax.broadcasted_iota(jnp.int32, (chunk, tile), 0)
                qp = pos0 + lax.shift_right_logical(
                    lax.broadcasted_iota(jnp.int32, (chunk, tile), 1), shift
                )
                s = jnp.where(kp <= qp, s, very_low)
            new = jnp.maximum(m, jnp.max(s, axis=0, keepdims=True))
            e = jnp.exp2(s - new)
            dp = dot_nt(v_sc[pl.ds(base, chunk), :], do)
            a = jnp.exp2(m - new)
            l = l * a + jnp.sum(e, axis=0, keepdims=True)
            dl = dl * a + jnp.sum(e * dp, axis=0, keepdims=True)
            e_sc[pl.ds(base, chunk), :] = e
            p_sc[pl.ds(base, chunk), :] = dp
            m_sc[pl.ds(c, 1), :] = new
            return new, l, dl

        init = (
            jnp.full((1, tile), very_low, F32),
            jnp.zeros((1, tile), F32),
            jnp.zeros((1, tile), F32),
        )
        carry = lax.fori_loop(0, nfull, lambda c, x: scores(c, x, False), init)
        m, l, dl = scores(nfull, carry, True)
        inv = 1.0 / l
        delta = dl * inv

        def grads(c, acc):
            base = pl.multiple_of(c * chunk, chunk)
            f = jnp.exp2(m_sc[pl.ds(c, 1), :] - m) * inv
            p = e_sc[pl.ds(base, chunk), :] * f
            ds = (p * (p_sc[pl.ds(base, chunk), :] - delta)).astype(BF16)
            dk_sc[pl.ds(base, chunk), :] += dot_nn(ds, q)
            dv_sc[pl.ds(base, chunk), :] += dot_nn(p.astype(BF16), do)
            return acc + dot_tn(k_sc[pl.ds(base, chunk), :], ds)

        acc = lax.fori_loop(0, nfull + 1, grads, jnp.zeros((head_size, tile), F32))
        return (acc * scaling).T.astype(BF16)

    cut = rows * half // 2

    def put(dq):
        @pl.when(part == 0)
        def _():
            dq_ref[0, 0, 0, :cut, :] = dq[:cut]
            dq_ref[1, 0, 0, :cut, :] = dq[cut:]

        @pl.when(part > 0)
        def _():
            dq_ref[part - 1, 0, 0, cut:, :] = dq

    @pl.when(live)
    def _():
        put(run())

    @pl.when(jnp.logical_not(live))
    def _():
        put(jnp.zeros((tile, head_size), BF16))

    @pl.when(step == slots * per_slot - 1)
    def _():
        for j in range(blocks):
            at = pl.multiple_of(order[j] * rows, rows)
            dkv_ref[j, 0, 0, :rows, :] = (dk_sc[pl.ds(at, rows), :] * scaling).astype(BF16)
            dkv_ref[j, 1, 0, :rows, :] = dv_sc[pl.ds(at, rows), :].astype(BF16)
            dkv_ref[j, 0, 0, rows:, :] = (
                dk_sc[pl.ds(total + j * rows, rows), :] * scaling
            ).astype(BF16)
            dkv_ref[j, 1, 0, rows:, :] = dv_sc[pl.ds(total + j * rows, rows), :].astype(BF16)


def attention(order, lengths, qp, qr, dop, dor, key_value, head, first_block, side):
    slots, tile, size = qp.shape[1:]
    full_rows = qr.shape[2]
    blocks, _, heads, double, _ = key_value.shape
    rows = double // 2
    half = tile // rows
    full = full_rows // rows
    keys = blocks * double
    chunk = min(512, keys // 2)
    per_slot = 1 + full // half
    kern = functools.partial(
        attn_kernel,
        blocks=blocks,
        slots=slots,
        rows=rows,
        half=half,
        full=full,
        chunk=chunk,
        first_block=first_block,
        side=side,
    )
    out_rows = rows // 2 * (half + full)
    q_pref = pl.BlockSpec((1, 1, tile, size), lambda h, t, *_: (head + h, t // per_slot, 0, 0))
    q_resp = pl.BlockSpec(
        (1, 1, tile, size),
        lambda h, t, *_: (head + h, t // per_slot, jnp.maximum(t % per_slot - 1, 0), 0),
    )
    kv_spec = pl.BlockSpec((blocks, 2, 1, double, size), lambda h, t, *_: (0, 0, h, 0, 0))
    spec = pltpu.PrefetchScalarGridSpec(
        num_scalar_prefetch=2,
        grid=(heads, slots * per_slot),
        in_specs=[q_pref, q_resp, q_pref, q_resp, kv_spec],
        out_specs=[
            pl.BlockSpec(
                (2, 1, 1, out_rows, size), lambda h, t, *_: (0, t // per_slot, h, 0, 0)
            ),
            kv_spec,
        ],
        scratch_shapes=[
            pltpu.VMEM((tile, size), BF16),
            pltpu.VMEM((tile, size), BF16),
            pltpu.VMEM((keys, size), BF16),
            pltpu.VMEM((keys, size), BF16),
            pltpu.VMEM((keys, size), F32),
            pltpu.VMEM((keys, size), F32),
            pltpu.VMEM((keys, tile), F32),
            pltpu.VMEM((keys, tile), F32),
            pltpu.VMEM((keys // chunk, tile), F32),
        ],
    )
    work = heads * slots * per_slot * tile * keys
    return pl.pallas_call(
        kern,
        grid_spec=spec,
        out_shape=[
            jax.ShapeDtypeStruct((2, slots, heads, out_rows, size), BF16),
            jax.ShapeDtypeStruct(key_value.shape, BF16),
        ],
        compiler_params=pltpu.CompilerParams(vmem_limit_bytes=48 << 20),
        cost_estimate=pl.CostEstimate(
            flops=10 * work * size, bytes_accessed=8 * work // keys * size, transcendentals=work
        ),
    )(order, lengths, qp, qr, dop, dor, key_value)


def split_heads(array):
    rows, heads, group, size = array.shape
    return array.transpose(1, 0, 2, 3).reshape(heads, rows * group, size)


def on_device(
    prefix_query_rows,
    prefix_key_rows,
    prefix_value_rows,
    prefix_output_gradient,
    resp_q,
    resp_k,
    response_value_rows,
    response_output_gradient,
    lengths,
    prefix_order,
    *,
    swap,
):
    chips = lax.axis_size("z")
    cores = lax.axis_size("core")
    parts = lax.axis_size("head")
    rows, local_heads, half, size = prefix_query_rows.shape
    full = resp_q.shape[3]
    key_value = jnp.stack(
        [
            jnp.concatenate([prefix_key_rows, resp_k[0]], axis=0),
            jnp.concatenate([prefix_value_rows, response_value_rows[0]], axis=0),
        ]
    ).transpose(2, 0, 1, 3)
    arrays = [
        split_heads(prefix_query_rows),
        split_heads(resp_q[0]),
        split_heads(prefix_output_gradient),
        split_heads(response_output_gradient[0]),
    ]
    side = lambda: lax.axis_index("pair")
    slots = cores if swap else 1
    heads = local_heads // slots
    if swap:
        key_value = lax.all_to_all(key_value, "core", 0, 1, tiled=True)
        arrays = [lax.all_to_all(a, "core", 0, 1, tiled=True) for a in arrays]
        first_block = lambda: lax.axis_index("z") * cores
        over = "z"
    else:
        first_block = lambda: lax.axis_index("z") * cores + lax.axis_index("core")
        over = ("z", "core")
    arrays = [a.reshape(heads, slots, -1, size) for a in arrays]
    gathered = [
        lax.all_gather(key_value[g].reshape(slots, 2, 1, 2 * rows, size), over, axis=0, tiled=True)
        for g in range(heads)
    ]
    dqs = []
    dkvs = []
    for g in range(heads):
        dq, dkv = attention(
            prefix_order, lengths, *arrays, gathered[g], g, first_block, side
        )
        dkvs.append(lax.psum_scatter(dkv, over, scatter_dimension=0, tiled=True))
        dqs.append(dq)
    return finish(dqs, dkvs, rows, half, full, size, slots, parts, swap)


def finish(dqs, dkvs, rows, half, full, size, slots, parts, swap):
    heads = len(dqs)
    part = rows // parts
    axes = ("head", "core") if swap else "head"
    sources = parts * slots

    def exchange(array):
        return lax.all_to_all(array, axes, 0, 0, tiled=True)

    pref = []
    resp = []
    cut = rows * half // 2
    for dq in dqs:
        dq = dq.reshape(2, slots, -1, size)
        if parts == 2:
            got = exchange(dq.reshape(sources, -1, size))
            pref.append(got[:, :cut].reshape(sources, part, half, size))
            resp.append(got[:, cut:].reshape(sources, part, full, size))
        else:
            a = dq[:, 0, :cut].reshape(sources, part * half, size)
            b = dq[:, 0, cut:].reshape(sources, part * full, size)
            pref.append(exchange(a).reshape(sources, part, half, size))
            resp.append(exchange(b).reshape(sources, part, full, size))
    dq_pref = jnp.stack(pref, 1).transpose(2, 0, 1, 3, 4).reshape(part, -1, half, size)
    dq_resp = jnp.stack(resp, 1).transpose(2, 0, 1, 3, 4).reshape(part, -1, full, size)
    out = []
    sums = []
    for dkv in dkvs:
        dkv = dkv.reshape(slots, 2, 2, rows, size)
        own = dkv[:, :, 0]
        other = lax.ppermute(own, "pair", [(0, 1), (1, 0)])
        own = (own.astype(F32) + other.astype(F32)).astype(BF16)
        both = jnp.stack([own, dkv[:, :, 1]], axis=2)
        both = both.reshape(slots, 2, 2, parts, part, size)
        sums.append(both.transpose(3, 0, 1, 2, 4, 5))
    all_sums = jnp.stack(sums, axis=2)
    got = exchange(all_sums.reshape((sources,) + all_sums.shape[2:]))
    got = got.transpose(2, 3, 4, 0, 1, 5).reshape(2, 2, part, sources * heads, size)
    return (
        dq_pref,
        got[0, 0],
        got[1, 0],
        dq_resp[None],
        got[0, 1][None],
        got[1, 1][None],
    )


def solution(mesh):
    sizes = mesh.shape
    fine = Mesh(
        mesh.devices.reshape(sizes["blk"] // 2, 2, sizes["pair"], sizes["head"]),
        ("z", "core", "pair", "head"),
    )
    blk = ("z", "core")
    in_specs = (
        P(blk, "head", "pair", None),
        P(blk, "head", None),
        P(blk, "head", None),
        P(blk, "head", "pair", None),
        P("pair", blk, "head", None, None),
        P("pair", blk, "head", None),
        P("pair", blk, "head", None),
        P("pair", blk, "head", None, None),
        P(),
        P(),
    )
    rows = ("z", "core", "head")
    out_specs = (
        P(rows, None, "pair", None),
        P(rows, None, None),
        P(rows, None, None),
        P("pair", rows, None, None, None),
        P("pair", rows, None, None),
        P("pair", rows, None, None),
    )

    def run(*args):
        local_heads = args[1].shape[1] // sizes["head"]
        body = functools.partial(on_device, swap=local_heads % 2 == 0 and sizes["head"] == 2)
        return jax.shard_map(
            body, mesh=fine, in_specs=in_specs, out_specs=out_specs, check_vma=False
        )(*args)

    return run
```

time: 365 us -> 163 us (0.45)
  matrix products: 116 us -> 0 us
  waiting for transfers between devices: 118 us -> 39.5 us
  other arithmetic: 57.8 us -> 0.74 us
  Pallas kernels: 0 us -> 37.4 us
  local copies, waits for them, and re-layouts: 20.7 us -> 26.3 us
  starting transfers between devices: 20.8 us -> 25.2 us
    dot_general x5 -> x0, matrix products: 116 us -> none  [the longest x1 40 us: scores_of(): jnp.einsum('gqd,gkd->gqk', grad_outs, pieces[1], preferred_element_type=j...]
    reduce_scatter x1 -> x2, waiting for transfers between devices: 68.1 us -> 16.3 us  [on_device(): dkvs.append(lax.psum_scatter(dkv, over, scatter_dimension=0, tiled=True))]
    convert_element_type x1 -> x2, other arithmetic: 41.1 us -> 0.08 us  [finish(): own = (own.astype(F32) + other.astype(F32)).astype(BF16)]
    pallas_call x0 -> x2, Pallas kernels: none -> 37.4 us  [attention(): pl.pallas_call(kern, grid_spec=spec, out_shape=[jax.ShapeDtypeStruct((2,...]
    all_gather x1 -> x2, waiting for transfers between devices: 38.2 us -> 12.4 us  [on_device(): lax.all_gather(key_value[g].reshape(slots, 2, 1, 2 * rows, size), over, a...]
    all_to_all x0 -> x2, blocking collectives: none -> 18.3 us  [the longest x1 14.2 us: exchange(): return lax.all_to_all(array, axes, 0, 0, tiled=True)]
    psum x1 -> x0, blocking collectives: 15.8 us -> none  [on_device(): summed = lax.psum(pref_grads, 'pair').astype(jnp.bfloat16)]
    unnamed x12 -> x42, local copies, waits for them, and re-layouts: 3.93 us -> 15.2 us
  transfers between devices with their start and end apart: 8 -> 12, of which waited for: 6 -> 8; matrix products, arithmetic and copies ran while one was open for 10% -> 8% of each run, Pallas kernels for 0% -> 23%
where the time goes in v1:
time: 163 us; the launch traced here: 161 us
  waiting for transfers between devices  39.5 us (24%)
  Pallas kernels  37.4 us (23%)
  local copies, waits for them, and re-layouts  26.3 us (16%)
  starting transfers between devices  25.2 us (15%)
  blocking collectives  18.3 us (11%)
  between operations  14.1 us (9%)
    pallas_call x2, Pallas kernels, attention(): pl.pallas_call(kern, grid_spec=spec, out_shape=[jax.ShapeDtypeStruct((2,...  37.4 us
    reduce_scatter x2, waiting for transfers between devices, on_device(): dkvs.append(lax.psum_scatter(dkv, over, scatter_dimension=0, tiled=True))  16.3 us
    unnamed x42, local copies, waits for them, and re-layouts  15.2 us
    all_to_all x4, starting transfers between devices, on_device(): arrays = [lax.all_to_all(a, 'core', 0, 1, tiled=True) for a in arrays]  15 us
    all_to_all x1, blocking collectives, exchange(): return lax.all_to_all(array, axes, 0, 0, tiled=True)  14.2 us
    all_gather x2, waiting for transfers between devices, on_device(): lax.all_gather(key_value[g].reshape(slots, 2, 1, 2 * rows, size), over, a...  12.4 us
    all_to_all x2, starting transfers between devices, exchange(): return lax.all_to_all(array, axes, 0, 0, tiled=True)  6.96 us
    all_to_all x2, waiting for transfers between devices, exchange(): return lax.all_to_all(array, axes, 0, 0, tiled=True)  5.07 us
  transfers between devices with their start and end apart: 12, of which 8 were waited for; matrix products, arithmetic and copies ran while one was open for 8% of the time, Pallas kernels for 23%

profile of v1, /device:TPU:0, one launch (start us, length us, event | category | flops | bytes accessed | tf_op | source)
XLA Modules:
  0.0 161.5 jit_solution(15330470964102043968)
XLA Ops:
  7.2 1.0 copy.118
  8.2 0.9 copy-done.14
  9.1 0.9 copy-done.15
  10.1 4.2 %all_to_all.90 = bf16[4,2,256,128]{3,2,1,0:T(8,128)(2,1)S(1)} all-to-all(bf16[4,2,256,128]{3,2,1,0:T(8,128)(2,1)S(1)} %maximum_bitcast_fusion), channel_id=1, replica_groups=mesh['z'=4,'core'=2,'pair'=2,'head'=2] {'core'}, dimensions={0} | all-to-all | bytes 1048576 | tf_op jit(solution)/shard_map/all_to_all | solution.py:279
  14.3 0.8 fusion
  15.2 0.7 all-gather.7.cloned.1.call-update
  15.9 1.2 copy.113
  17.1 3.7 %all-to-all-start.3 = ((bf16[4,1024,128]{2,1,0:T(8,128)(2,1)}), bf16[4,1024,128]{2,1,0:T(8,128)(2,1)S(1)}, u32[]{:S(2)}, u32[]{:S(2)}) async-start(bf16[4,1024,128]{2,1,0:T(8,128)(2,1)} %bitcast.97), calls=%async_computation.3 | async-start | bytes 2097152 | tf_op jit(solution)/shard_map/all_to_all | solution.py:280
  20.8 1.2 copy.115
  22.0 0.9 all-to-all-done.3
  22.9 3.6 %all-to-all-start.1 = ((bf16[4,1024,128]{2,1,0:T(8,128)(2,1)}), bf16[4,1024,128]{2,1,0:T(8,128)(2,1)S(1)}, u32[]{:S(2)}, u32[]{:S(2)}) async-start(bf16[4,1024,128]{2,1,0:T(8,128)(2,1)} %bitcast.99), calls=%async_computation.1 | async-start | bytes 2097152 | tf_op jit(solution)/shard_map/all_to_all | solution.py:280
  26.6 1.0 copy-done.11
  27.6 1.0 copy.74
  28.6 4.2 %all-to-all-start.2 = ((bf16[4,512,128]{2,1,0:T(8,128)(2,1)}), bf16[4,512,128]{2,1,0:T(8,128)(2,1)}, u32[]{:S(2)}, u32[]{:S(2)}) async-start(bf16[4,512,128]{2,1,0:T(8,128)(2,1)} %bitcast.10), calls=%async_computation.2 | async-start | bytes 1048576 | tf_op jit(solution)/shard_map/all_to_all | solution.py:280
  32.9 1.0 copy-done.12
  33.9 1.0 copy.70
  34.9 3.5 %all-to-all-start = ((bf16[4,512,128]{2,1,0:T(8,128)(2,1)}), bf16[4,512,128]{2,1,0:T(8,128)(2,1)S(1)}, u32[]{:S(2)}, u32[]{:S(2)}) async-start(bf16[4,512,128]{2,1,0:T(8,128)(2,1)} %bitcast.1), calls=%async_computation | async-start | bytes 1048576 | tf_op jit(solution)/shard_map/all_to_all | solution.py:280
  38.4 1.1 copy.116
  39.5 0.6 all-to-all-done
  40.1 0.8 copy.117
  40.9 5.1 %all-gather.5.cloned.1.call-done = bf16[1,8,2,256,128]{4,3,2,0,1:T(8,128)(2,1)} async-done(((bf16[1,2,2,256,128]{4,3,2,0,1:T(8,128)(2,1)}), bf16[1,8,2,256,128]{4,3,2,0,1:T(8,128)(2,1)}) %all-gather.5.cloned.1.call-update) | async-done | bytes 1048592 | tf_op jit(solution)/shard_map/all_gather | solution.py:288
  46.0 0.7 copy-done.4
  46.7 1.0 copy-done
  47.7 1.2 copy-done.3
  49.0 18.6 %shard_map.145 = (bf16[2,2,1,768,128]{4,3,2,1,0:T(8,128)(2,1)S(1)}, bf16[8,2,1,256,128]{4,3,2,1,0:T(8,128)(2,1)}) custom-call(s32[8]{0:T(128)S(1)} %copy-done.4, s32[2]{0:T(128)S(1)} %copy-done.5, bf16[2,2,512,128]{3,2,1,0:T(8,128)(2,1)S(1)} %bitcast.111, bf16[2,2,1024,128]{3,2,1,0:T(8,128)(2,1)S(1)} %bitcast.106, bf16[2,2,512,128]{3,2,1,0:T(8,128)(2,1)S(1)} %bitcast.109, ...), custom_call_target="tpu_custom_call" | custom-call | flops 8053063680 | bytes 3145728 | tf_op jit(solution)/shard_map/pallas_call | solution.py:225
  67.6 7.3 %all-gather.7.cloned.1.call-done = bf16[1,8,2,256,128]{4,3,2,0,1:T(8,128)(2,1)} async-done(((bf16[1,2,2,256,128]{4,3,2,0,1:T(8,128)(2,1)}), bf16[1,8,2,256,128]{4,3,2,0,1:T(8,128)(2,1)}) %all-gather.7.cloned.1.call-update) | async-done | bytes 1048592 | tf_op jit(solution)/shard_map/all_gather | solution.py:288
  75.0 1.0 copy-done.1
  76.0 1.2 copy-done.2
  77.2 18.7 %shard_map.146 = (bf16[2,2,1,768,128]{4,3,2,1,0:T(8,128)(2,1)}, bf16[8,2,1,256,128]{4,3,2,1,0:T(8,128)(2,1)}) custom-call(s32[8]{0:T(128)S(1)} %copy-done.4, s32[2]{0:T(128)S(1)} %copy-done.5, bf16[2,2,512,128]{3,2,1,0:T(8,128)(2,1)S(1)} %bitcast.112, bf16[2,2,1024,128]{3,2,1,0:T(8,128)(2,1)S(1)} %bitcast.107, bf16[2,2,512,128]{3,2,1,0:T(8,128)(2,1)S(1)} %bitcast.110, ...), custom_call_target="tpu_custom_call" | custom-call | flops 8053063680 | bytes 3145728 | tf_op jit(solution)/shard_map/pallas_call | solution.py:225
  96.0 14.2 %all_to_all.91 = bf16[4,768,128]{2,1,0:T(8,128)(2,1)S(1)} all-to-all(bf16[4,768,128]{2,1,0:T(8,128)(2,1)S(1)} %bitcast.108), channel_id=1, replica_groups=mesh['z'=4,'core'=2,'pair'=2,'head'=2] {'head','core'}, dimensions={0} | all-to-all | bytes 1572864 | tf_op jit(solution)/shard_map/all_to_all | solution.py:309
  110.2 3.5 %all-to-all-start.6 = ((bf16[4,768,128]{2,1,0:T(8,128)(2,1)}), bf16[4,768,128]{2,1,0:T(8,128)(2,1)S(1)}, u32[]{:S(2)}, u32[]{:S(2)}) async-start(bf16[4,768,128]{2,1,0:T(8,128)(2,1)} %bitcast.30), calls=%async_computation.6 | async-start | bytes 1572864 | tf_op jit(solution)/shard_map/all_to_all | solution.py:309
  113.8 1.0 slice_bitcast_fusion.7
  114.7 1.5 collective-permute-start
  116.3 16.2 %reduce-scatter.5.cloned.1.call-done = bf16[2,2,1,256,128]{4,3,2,1,0:T(8,128)(2,1)} async-done(((bf16[8,2,1,256,128]{4,3,2,1,0:T(8,128)(2,1)}), bf16[2,2,1,256,128]{4,3,2,1,0:T(8,128)(2,1)}) %reduce-scatter.5.cloned.1.call-update) | async-done | bytes 262160 | tf_op jit(solution)/shard_map/reduce_scatter | solution.py:297
  132.5 1.0 slice_bitcast_fusion.6
  133.6 1.5 collective-permute-start.1
  135.2 3.4 %collective-permute-done.1 = bf16[2,2,128,128]{3,2,1,0:T(8,128)(2,1)S(1)} collective-permute-done((bf16[2,2,128,128]{3,2,1,0:T(8,128)(2,1)S(1)}, bf16[2,2,128,128]{3,2,1,0:T(8,128)(2,1)S(1)}, u32[]{:S(2)}, u32[]{:S(2)}) %collective-permute-start.1) | collective-permute-done | bytes 131104 | tf_op jit(solution)/shard_map/ppermute | solution.py:332
  138.8 0.8 copy.90
  139.6 3.5 %all-to-all-start.7 = ((bf16[4,2,2,2,64,128]{5,4,3,2,1,0:T(8,128)(2,1)}), bf16[4,2,2,2,64,128]{5,4,3,2,1,0:T(8,128)(2,1)S(1)}, u32[]{:S(2)}, u32[]{:S(2)}) async-start(bf16[4,2,2,2,64,128]{5,4,3,2,1,0:T(8,128)(2,1)} %copy.90), calls=%async_computation.9 | async-start | bytes 1048576 | tf_op jit(solution)/shard_map/all_to_all | solution.py:309
  143.2 1.3 copy.99
  144.5 0.9 slice-done
  145.5 0.4 pad_maximum_fusion.1
  145.8 1.0 copy.98
  146.8 5.1 %all-to-all-done.7 = bf16[4,2,2,2,64,128]{5,4,3,2,1,0:T(8,128)(2,1)S(1)} async-done(((bf16[4,2,2,2,64,128]{5,4,3,2,1,0:T(8,128)(2,1)}), bf16[4,2,2,2,64,128]{5,4,3,2,1,0:T(8,128)(2,1)S(1)}, u32[]{:S(2)}, u32[]{:S(2)}) %all-to-all-start.7) | async-done | bytes 524320 | tf_op jit(solution)/shard_map/all_to_all | solution.py:309
  152.0 0.7 copy.94
  152.7 0.7 copy.95
  153.5 0.7 copy.96
  154.2 0.7 copy.97
  (56 shorter events, 1.1 us)
Async XLA Ops:
  7.2 1.0 copy-start.13
  7.2 38.8 %all-gather.5.cloned.1.call-start = ((), (), s32[]{:S(2)}) async-start(), calls=%async_computation.12 | async-start | bytes 1310720 | tf_op jit(solution)/shard_map/all_gather | solution.py:288
  8.2 0.9 copy-start.14
  9.1 0.9 copy-start.15
  14.3 1.6 %copy-start.7 = (bf16[1,128,4,8,128]{4,3,2,1,0:T(8,128)(2,1)S(1)}, bf16[1,128,4,8,128]{4,3,2,1,0:T(8,128)(2,1)}, u32[]{:S(2)}) copy-start(bf16[1,128,4,8,128]{4,3,2,1,0:T(8,128)(2,1)} %param.17) | copy-start | bytes 3145732
  15.1 59.8 %all-gather.7.cloned.1.call-start = ((), (), s32[]{:S(2)}) async-start(), calls=%async_computation.13 | async-start | bytes 1310720 | tf_op jit(solution)/shard_map/all_gather | solution.py:288
  17.1 3.7 %copy-start.8 = (bf16[1,128,4,8,128]{4,3,2,1,0:T(8,128)(2,1)S(1)}, bf16[1,128,4,8,128]{4,3,2,1,0:T(8,128)(2,1)}, u32[]{:S(2)}) copy-start(bf16[1,128,4,8,128]{4,3,2,1,0:T(8,128)(2,1)} %param.14) | copy-start | bytes 3145732
  17.1 5.8 %all-to-all-start.3 = ((bf16[4,1024,128]{2,1,0:T(8,128)(2,1)}), bf16[4,1024,128]{2,1,0:T(8,128)(2,1)S(1)}, u32[]{:S(2)}, u32[]{:S(2)}) async-start(bf16[4,1024,128]{2,1,0:T(8,128)(2,1)} %bitcast.97), calls=%async_computation.3 | async-start | bytes 2097152 | tf_op jit(solution)/shard_map/all_to_all | solution.py:280
  22.9 5.7 %all-to-all-start.1 = ((bf16[4,1024,128]{2,1,0:T(8,128)(2,1)}), bf16[4,1024,128]{2,1,0:T(8,128)(2,1)S(1)}, u32[]{:S(2)}, u32[]{:S(2)}) async-start(bf16[4,1024,128]{2,1,0:T(8,128)(2,1)} %bitcast.99), calls=%async_computation.1 | async-start | bytes 2097152 | tf_op jit(solution)/shard_map/all_to_all | solution.py:280
  26.5 1.0 copy-start.11
  28.6 6.3 %all-to-all-start.2 = ((bf16[4,512,128]{2,1,0:T(8,128)(2,1)}), bf16[4,512,128]{2,1,0:T(8,128)(2,1)}, u32[]{:S(2)}, u32[]{:S(2)}) async-start(bf16[4,512,128]{2,1,0:T(8,128)(2,1)} %bitcast.10), calls=%async_computation.2 | async-start | bytes 1048576 | tf_op jit(solution)/shard_map/all_to_all | solution.py:280
  32.8 1.1 copy-start.12
  34.9 5.2 %all-to-all-start = ((bf16[4,512,128]{2,1,0:T(8,128)(2,1)}), bf16[4,512,128]{2,1,0:T(8,128)(2,1)S(1)}, u32[]{:S(2)}, u32[]{:S(2)}) async-start(bf16[4,512,128]{2,1,0:T(8,128)(2,1)} %bitcast.1), calls=%async_computation | async-start | bytes 1048576 | tf_op jit(solution)/shard_map/all_to_all | solution.py:280
  38.4 75.4 %reduce-scatter.3.cloned.1.call-start = ((), (), s32[]{:S(2)}) async-start(), calls=%async_computation.10 | async-start | bytes 1310720 | tf_op jit(solution)/shard_map/reduce_scatter | solution.py:297
  46.0 0.7 copy-start.4
  46.0 0.7 copy-start.5
  46.7 1.0 copy-start
  47.7 1.2 copy-start.3
  67.6 64.9 %reduce-scatter.5.cloned.1.call-start = ((), (), s32[]{:S(2)}) async-start(), calls=%async_computation.11 | async-start | bytes 1310720 | tf_op jit(solution)/shard_map/reduce_scatter | solution.py:297
  75.0 1.0 copy-start.1
  76.0 1.2 copy-start.2
  110.2 34.3 %copy-start.6 = (bf16[4,768,128]{2,1,0:T(8,128)(2,1)}, bf16[4,768,128]{2,1,0:T(8,128)(2,1)S(1)}, u32[]{:S(2)}) copy-start(bf16[4,768,128]{2,1,0:T(8,128)(2,1)S(1)} %all_to_all.91) | copy-start | bytes 2359300
  110.2 29.4 %all-to-all-start.6 = ((bf16[4,768,128]{2,1,0:T(8,128)(2,1)}), bf16[4,768,128]{2,1,0:T(8,128)(2,1)S(1)}, u32[]{:S(2)}, u32[]{:S(2)}) async-start(bf16[4,768,128]{2,1,0:T(8,128)(2,1)} %bitcast.30), calls=%async_computation.6 | async-start | bytes 1572864 | tf_op jit(solution)/shard_map/all_to_all | solution.py:309
  114.7 20.4 %collective-permute-start = (bf16[2,2,128,128]{3,2,1,0:T(8,128)(2,1)S(1)}, bf16[2,2,128,128]{3,2,1,0:T(8,128)(2,1)S(1)}, u32[]{:S(2)}, u32[]{:S(2)}) collective-permute-start(bf16[2,2,128,128]{3,2,1,0:T(8,128)(2,1)S(1)} %get-tuple-element.32), channel_id=1, source_target_pairs={{0,2},{2,0},{1,3},{3,1},{4,6},{6,4},{5,7},{7,5},{8,10},{10,8},{9,1... | collective-permute-start | bytes 393224 | tf_op jit(solution)/shard_map/ppermute | solution.py:332
  132.5 2.6 %copy-start.9 = (bf16[2,2,1,256,128]{4,3,2,1,0:T(8,128)(2,1)S(1)}, bf16[2,2,1,256,128]{4,3,2,1,0:T(8,128)(2,1)}, u32[]{:S(2)}) copy-start(bf16[2,2,1,256,128]{4,3,2,1,0:T(8,128)(2,1)} %reduce-scatter.3.cloned.1.call-done) | copy-start | bytes 786436
  133.6 5.0 %collective-permute-start.1 = (bf16[2,2,128,128]{3,2,1,0:T(8,128)(2,1)S(1)}, bf16[2,2,128,128]{3,2,1,0:T(8,128)(2,1)S(1)}, u32[]{:S(2)}, u32[]{:S(2)}) collective-permute-start(bf16[2,2,128,128]{3,2,1,0:T(8,128)(2,1)S(1)} %get-tuple-element.34), channel_id=1, source_target_pairs={{0,2},{2,0},{1,3},{3,1},{4,6},{6,4},{5,7},{7,5},{8,10},{10,8},{9,1... | collective-permute-start | bytes 393224 | tf_op jit(solution)/shard_map/ppermute | solution.py:332
  135.2 3.4 %copy-start.10 = (bf16[2,2,1,256,128]{4,3,2,1,0:T(8,128)(2,1)S(1)}, bf16[2,2,1,256,128]{4,3,2,1,0:T(8,128)(2,1)}, u32[]{:S(2)}) copy-start(bf16[2,2,1,256,128]{4,3,2,1,0:T(8,128)(2,1)} %reduce-scatter.5.cloned.1.call-done) | copy-start | bytes 786436
  139.6 12.3 %all-to-all-start.7 = ((bf16[4,2,2,2,64,128]{5,4,3,2,1,0:T(8,128)(2,1)}), bf16[4,2,2,2,64,128]{5,4,3,2,1,0:T(8,128)(2,1)S(1)}, u32[]{:S(2)}, u32[]{:S(2)}) async-start(bf16[4,2,2,2,64,128]{5,4,3,2,1,0:T(8,128)(2,1)} %copy.90), calls=%async_computation.9 | async-start | bytes 1048576 | tf_op jit(solution)/shard_map/all_to_all | solution.py:309
  144.5 1.0 slice-start
Sparse Core Ops, SparseCore 0:
  15.3 30.6 all-gather.4
  47.6 27.3 all-gather.6
  77.3 26.6 reduce-scatter.2
  106.7 25.7 reduce-scatter.4
